TPU v7x, 32 devices: a whole 2x2x4 slice. The times are simulated.
32 devices in a mesh: dp: 2 (over x), ctx: 8 (over z, y), head: 2 (over core).
Axes of the slice: x: 2, y: 2, z: 4, core: 2. Of those that a mesh axis runs over, the one named last changes fastest.
Arguments:
- queries: bfloat16 [2, 1024, 4096], P('dp', 'ctx', 'head'), may hold values from -200 to 200
- targets: bfloat16 [2, 1024, 4096], P('dp', 'ctx', 'head'), may hold values from -3 to 3
- document_keys: bfloat16 [2, 1024, 256], P('dp', 'ctx', 'head'), may hold values from -6 to 6
- document_values: bfloat16 [2, 1024, 256], P('dp', 'ctx', 'head'), may hold values from -6 to 6
- doc_pos: int32 [2, 1024], P('dp', 'ctx'), may hold values from 0 to 1023, each once within a row
- cart_keys: bfloat16 [128, 256], P('ctx', 'head'), may hold values from -8 to 8
- cartridge_values: bfloat16 [128, 256], P('ctx', 'head'), may hold values from -6 to 6
- master: float32 [128, 2, 256], P('ctx', 'head', 'dp'), may hold values from -5 to 5
- first_moment1: float32 [128, 2, 256], P('ctx', 'head', 'dp'), may hold values from -4 to 4
- second_moment2: float32 [128, 2, 256], P('ctx', 'head', 'dp'), may hold values from 0.1 to 2
Outputs:
- new_out: bfloat16 [2, 1024, 4096], P('dp', 'ctx', 'head')
- new_master: float32 [128, 2, 256], P('ctx', 'head', 'dp')
- new_moment1: float32 [128, 2, 256], P('ctx', 'head', 'dp')
- new_moment2: float32 [128, 2, 256], P('ctx', 'head', 'dp')
Inputs may be any that keep to these rules, and one draw needn't show every extreme that they name: Each row of doc_pos holds every position of the document once.
All inputs are finite; a program needn't handle non-finite values.
Results may differ from a plain program's by a relative error of at most 0.015.
Values may be sent and summed in bfloat16 or wider, within the bound.
No kernel may reach another device: no remote copies, remote signals or barrier semaphores. Data moves between devices by JAX's collectives and lax.ppermute only.
A program may use at most 64 MiB of HBM per device.

v0:
```python
import math
import jax
import jax.numpy as jnp
from jax import lax
from jax.sharding import PartitionSpec as P

beta_one = 0.8
beta_two = 0.95
learn_rate = 0.1
adam_eps = 1e-08
norm_eps = 1e-06
neg_big = -1e30


def scores_of(left, right):
    return lax.dot_general(
        left, right, (((1,), (1,)), ((), ())), preferred_element_type=jnp.float32
    )


def online(state, scores, values, allowed):
    old_top, old_total, old_acc = state
    if allowed is not None:
        scores = jnp.where(allowed, scores, neg_big)
    new_top = jnp.maximum(old_top, jnp.max(scores, axis=1))
    weights = jnp.exp(scores - new_top[:, None])
    if allowed is not None:
        weights = jnp.where(allowed, weights, 0.0)
    factor = jnp.exp(old_top - new_top)
    total = old_total * factor + jnp.sum(weights, axis=1)
    accum = old_acc * factor[:, None] + jnp.dot(
        weights.astype(jnp.bfloat16), values, preferred_element_type=jnp.float32
    )
    return (new_top, total, accum)


def combine(first, second):
    top = jnp.maximum(first[0], second[0])
    f_one = jnp.exp(first[0] - top)
    f_two = jnp.exp(second[0] - top)
    total = first[1] * f_one + second[1] * f_two
    accum = first[2] * f_one[:, None] + second[2] * f_two[:, None]
    return (top, total, accum)


def local(
    queries,
    targets,
    document_keys,
    document_values,
    doc_pos,
    cart_keys,
    cartridge_values,
    master,
    first_moment1,
    second_moment2,
):
    head_dim = document_keys.shape[2]
    rows = queries.shape[1]
    group = queries.shape[2] // head_dim
    scale = head_dim ** (-0.5)
    flat_query = queries[0].reshape(rows * group, head_dim)
    query_pos = jnp.repeat(doc_pos[0], group)
    all_pos = lax.all_gather(doc_pos[0], "ctx", axis=0, tiled=True)
    cart_k_all, cart_v_all = (
        lax.all_gather(cart_keys, "ctx", axis=0, tiled=True),
        lax.all_gather(cartridge_values, "ctx", axis=0, tiled=True),
    )
    empty = (
        jnp.full((rows * group,), neg_big, jnp.float32),
        jnp.zeros((rows * group,), jnp.float32),
        jnp.zeros((rows * group, head_dim), jnp.float32),
    )

    def cart_part(keys_all, values_all):
        return online(empty, scores_of(flat_query, keys_all) * scale, values_all, None)

    state = empty
    keys = lax.all_gather(document_keys, "ctx", axis=1, tiled=True)[0]
    values = lax.all_gather(document_values, "ctx", axis=1, tiled=True)[0]
    count = keys.shape[0]
    step_rows = math.gcd(count, 512)

    def inner(carry, index):
        first = index * step_rows
        key_block = lax.dynamic_slice_in_dim(keys, first, step_rows)
        value_block = lax.dynamic_slice_in_dim(values, first, step_rows)
        pos_block = lax.dynamic_slice_in_dim(all_pos, first, step_rows)
        allowed = pos_block[None, :] <= query_pos[:, None]
        scores = scores_of(flat_query, key_block) * scale
        return (online(carry, scores, value_block, allowed), None)

    state, _ = lax.scan(inner, state, jnp.arange(count // step_rows, dtype=jnp.int32))
    merged = combine(cart_part(cart_k_all, cart_v_all), state)
    top, total = (merged[0], merged[1])
    out = merged[2] / total[:, None]
    d_out = out - targets[0].reshape(rows * group, head_dim).astype(jnp.float32)
    delta = jnp.sum(d_out * out, axis=1)
    d_out_b = d_out.astype(jnp.bfloat16)
    width = master.shape[2]
    count_all = master.size * lax.axis_size("dp") * lax.axis_size("ctx") * lax.axis_size("head")
    probs = jnp.exp(scores_of(flat_query, cart_k_all) * scale - top[:, None]) / total[:, None]
    d_probs = scores_of(d_out_b, cart_v_all)
    d_scores = probs * (d_probs - delta[:, None])
    grad_k = (
        lax.dot_general(
            d_scores.astype(jnp.bfloat16),
            flat_query,
            (((0,), (0,)), ((), ())),
            preferred_element_type=jnp.float32,
        )
        * scale
    )
    grad_v = lax.dot_general(
        probs.astype(jnp.bfloat16),
        d_out_b,
        (((0,), (0,)), ((), ())),
        preferred_element_type=jnp.float32,
    )
    term = lax.psum_scatter(
        jnp.concatenate([grad_k, grad_v], axis=1).astype(jnp.bfloat16),
        "ctx",
        scatter_dimension=0,
        tiled=True,
    ).astype(jnp.float32)
    full = lax.psum(term, "dp")
    squares = lax.psum(jnp.sum(full * full), ("ctx", "head"))
    owned = lax.dynamic_slice_in_dim(full, lax.axis_index("dp") * width, width, 1)
    rms = jnp.sqrt(squares / count_all + norm_eps)
    normed = (owned / rms).reshape(master.shape)
    new_moment1 = beta_one * first_moment1 + (1.0 - beta_one) * normed
    new_moment2 = beta_two * second_moment2 + (1.0 - beta_two) * normed * normed
    new_master = master - learn_rate * new_moment1 / (jnp.sqrt(new_moment2) + adam_eps)
    copies = new_master.reshape(master.shape[0], width).astype(jnp.bfloat16)
    columns = lax.all_gather(copies, "dp", axis=1, tiled=True)
    fresh = lax.all_gather(columns, "ctx", axis=0, tiled=True)
    final = combine(cart_part(fresh[:, :head_dim], fresh[:, head_dim:]), state)
    new_out = (final[2] / final[1][:, None]).astype(jnp.bfloat16).reshape(1, rows, group * head_dim)
    return (new_out, new_master, new_moment1, new_moment2)


def solution(mesh):
    in_specs = (
        P("dp", "ctx", "head"),
        P("dp", "ctx", "head"),
        P("dp", "ctx", "head"),
        P("dp", "ctx", "head"),
        P("dp", "ctx"),
        P("ctx", "head"),
        P("ctx", "head"),
        P("ctx", "head", "dp"),
        P("ctx", "head", "dp"),
        P("ctx", "head", "dp"),
    )
    out_specs = (
        P("dp", "ctx", "head"),
        P("ctx", "head", "dp"),
        P("ctx", "head", "dp"),
        P("ctx", "head", "dp"),
    )
    return jax.shard_map(local, mesh=mesh, in_specs=in_specs, out_specs=out_specs, check_vma=False)
```

profile of v0, /device:TPU:0, one launch (start us, length us, event | category | flops | bytes accessed | tf_op | source)
XLA Modules:
  0.0 330.7 jit_solution(10116764384674142388)
XLA Ops:
  7.2 0.0 reduce-scatter.4.cloned.1.call-start
  7.2 22.5 %all-gather = s32[1,1024]{1,0:T(1,128)S(1)} all-gather(s32[1,128]{1,0:T(1,128)} %param.16), channel_id=2, replica_groups=mesh['dp'=2,'ctx'=8,'head'=2] {'ctx'}, dimensions={1}, use_global_device_ids=true | all-gather | bytes 4608 | tf_op jit(solution)/shard_map/all_gather | solution.py:64
  29.7 30.9 %all_gather.23 = bf16[1,1024,128]{2,1,0:T(8,128)(2,1)S(1)} all-gather(bf16[1,128,128]{2,1,0:T(8,128)(2,1)} %param.14), channel_id=1, replica_groups=mesh['dp'=2,'ctx'=8,'head'=2] {'ctx'}, dimensions={1}, use_global_device_ids=true | all-gather | bytes 294912 | tf_op jit(solution)/shard_map/all_gather | solution.py:79
  60.6 1.3 reshape_squeeze.4
  61.9 31.0 %all_gather.24 = bf16[1,1024,128]{2,1,0:T(8,128)(2,1)S(1)} all-gather(bf16[1,128,128]{2,1,0:T(8,128)(2,1)} %param.15), channel_id=1, replica_groups=mesh['dp'=2,'ctx'=8,'head'=2] {'ctx'}, dimensions={1}, use_global_device_ids=true | all-gather | bytes 294912 | tf_op jit(solution)/shard_map/all_gather | solution.py:80
  92.9 0.0 copy-start.1
  92.9 0.0 copy-start.5
  92.9 23.1 %while.15 = (s32[]{:T(128)}, f32[2048]{0:T(1024)S(1)}, f32[2048]{0:T(1024)S(1)}, f32[2048,128]{1,0:T(8,128)}, s32[2]{0:T(128)S(1)}, /*index=5*/s32[1024]{0:T(102...) while((s32[]{:T(128)}, f32[2048]{0:T(1024)S(1)}, ...), condition=%wide.region_4.5_spmd.clone, body=%wide.region_1.4_spmd.clone.sunk | while | flops 554444800 | bytes 32434936 | solution.py:93
  92.9 0.8 broadcast_in_dim.101
  93.7 0.1 le.61
  93.8 0.6 dynamic_slice.40
  95.0 0.1 dynamic_slice.41
  95.1 2.7 fusion.74
  97.8 0.0 copy-start
  97.8 3.5 %fusion.75 = f32[2048]{0:T(1024)S(1)} fusion(f32[512,2048]{1,0:T(8,128)} %get-tuple-element.222, f32[2048]{0:T(1024)S(1)} %select_maximum_fusion.2, s32[2048]{0:T(1024)S(1)} %le.61, s32[512]{0:T(512)S(1)} %dynamic_slice.41), kind=kLoop, calls=%fused_computation.6.clone.1 | loop fusion | flops 6289408 | bytes 4220928 | tf_op jit(solution)/shard_map/while/body/eval_jaxpr/reduce_sum | solution.py:30
  101.3 0.0 copy-done
  101.3 2.5 convolution_add_fusion.4
  103.9 0.7 broadcast_in_dim.101
  104.6 0.1 le.61
  104.7 0.6 dynamic_slice.40
  105.9 0.1 dynamic_slice.41
  106.0 2.7 fusion.74
  108.7 0.0 copy-start
  108.7 3.5 %fusion.75 = f32[2048]{0:T(1024)S(1)} fusion(f32[512,2048]{1,0:T(8,128)} %get-tuple-element.222, f32[2048]{0:T(1024)S(1)} %select_maximum_fusion.2, s32[2048]{0:T(1024)S(1)} %le.61, s32[512]{0:T(512)S(1)} %dynamic_slice.41), kind=kLoop, calls=%fused_computation.6.clone.1 | loop fusion | flops 6289408 | bytes 4220928 | tf_op jit(solution)/shard_map/while/body/eval_jaxpr/reduce_sum | solution.py:30
  112.2 0.0 copy-done
  112.2 3.8 %convolution_add_fusion.4 = f32[2048,128]{1,0:T(8,128)} fusion(f32[512,2048]{1,0:T(8,128)S(1)} %copy-done, f32[2048]{0:T(1024)S(1)} %select_maximum_fusion.2, s32[2048]{0:T(1024)S(1)} %le.61, s32[512]{0:T(512)S(1)} %dynamic_slice.41, f32[2048,128]{1,0:T(8,128)} %get-tuple-element.242, f32[2048]{0:T(1024)S(1)} %get-tuple-element.224, ...), kind=kOutput, calls=%fused_computation.4.clone.1 | convolution fusion | flops 275513344 | bytes 6449157 | tf_op jit(solution)/shard_map/while/body/eval_jaxpr/dot_general | solution.py:31
  116.0 0.0 copy-done.1
  116.0 0.0 copy-start.6
  116.0 0.2 reshape.48
  116.2 0.3 copy.47
  116.6 0.0 copy-done.5
  116.6 30.6 %all_gather.21 = bf16[128,128]{1,0:T(8,128)(2,1)S(1)} all-gather(bf16[16,128]{1,0:T(8,128)(2,1)S(1)} %copy-done.5), channel_id=1, replica_groups=mesh['dp'=2,'ctx'=8,'head'=2] {'ctx'}, dimensions={0}, use_global_device_ids=true | all-gather | bytes 36864 | tf_op jit(solution)/shard_map/all_gather | solution.py:66
  147.2 0.3 fusion.54
  147.5 2.6 copy.46
  150.0 0.0 copy-done.6
  150.0 30.6 %all_gather.25 = bf16[128,128]{1,0:T(8,128)(2,1)S(1)} all-gather(bf16[16,128]{1,0:T(8,128)(2,1)S(1)} %copy-done.6), channel_id=1, replica_groups=mesh['dp'=2,'ctx'=8,'head'=2] {'ctx'}, dimensions={0}, use_global_device_ids=true | all-gather | bytes 36864 | tf_op jit(solution)/shard_map/all_gather | solution.py:67
  180.6 0.2 fusion.34
  180.8 1.7 multiply_reduce_fusion
  182.6 0.0 copy-start.2
  182.6 0.0 copy-start.3
  182.6 0.0 copy-start.4
  182.6 0.4 convolution_convert_fusion
  183.0 0.6 fusion.32
  183.6 0.7 copy.56
  184.4 0.0 reduce-scatter.4.cloned.1.call-update
  184.4 59.8 %reduce-scatter.4.cloned.1.call-done = bf16[16,256]{1,0:T(8,128)(2,1)} async-done(((bf16[128,256]{1,0:T(8,128)(2,1)}), bf16[16,256]{1,0:T(8,128)(2,1)}) %reduce-scatter.4.cloned.1.call-update) | async-done | bytes 8208 | tf_op jit(solution)/shard_map/reduce_scatter | solution.py:120
  244.2 8.7 %psum.14 = f32[16,256]{1,0:T(8,128)S(1)} all-reduce(bf16[16,256]{1,0:T(8,128)(2,1)} %reduce-scatter.4.cloned.1.call-done), channel_id=1, replica_groups=mesh['dp'=2,'ctx'=8,'head'=2] {'dp'}, use_global_device_ids=true, to_apply=%region_8.9 | all-reduce | flops 4096 | bytes 24576 | tf_op jit(solution)/shard_map/psum | solution.py:126
  252.9 0.6 multiply_reduce_fusion.1
  253.5 30.1 %psum.15 = f32[]{:T(128)} all-reduce(f32[]{:T(128)} %multiply_reduce_fusion.1), channel_id=1, replica_groups=mesh['dp'=2,'ctx'=8,'head'=2] {'ctx','head'}, use_global_device_ids=true, to_apply=%region_10.11 | all-reduce | flops 1 | bytes 8 | tf_op jit(solution)/shard_map/psum | solution.py:127
  284.3 0.0 copy-done.2
  284.3 0.0 copy-done.3
  284.3 0.0 copy-done.4
  284.3 0.6 fusion.52
  285.0 4.3 %all-gather.1 = bf16[16,1,256]{2,0,1:T(8,128)(2,1)S(1)} all-gather(bf16[16,1,128]{2,0,1:T(8,128)(2,1)S(1)} %get-tuple-element.138), channel_id=3, replica_groups=mesh['dp'=2,'ctx'=8,'head'=2] {'dp'}, dimensions={2}, use_global_device_ids=true | all-gather | bytes 12288 | tf_op jit(solution)/shard_map/all_gather | solution.py:135
  289.3 30.5 %all-gather.2 = bf16[128,1,256]{2,0,1:T(8,128)(2,1)S(1)} all-gather(bf16[16,1,256]{2,0,1:T(8,128)(2,1)S(1)} %all-gather.1), channel_id=4, replica_groups=mesh['dp'=2,'ctx'=8,'head'=2] {'ctx'}, dimensions={0}, use_global_device_ids=true | all-gather | bytes 73728 | tf_op jit(solution)/shard_map/all_gather | solution.py:136
  319.8 0.3 fusion.55
  320.1 0.2 fusion.35
  320.3 2.5 fusion.28
  322.8 1.0 reshape.47
  (15 shorter events, 0.1 us)
Async XLA Ops:
  7.2 237.0 %reduce-scatter.4.cloned.1.call-start = ((), (), s32[]{:S(2)}) async-start(), calls=%async_computation.1 | async-start | bytes 73728 | tf_op jit(solution)/shard_map/reduce_scatter | solution.py:120
  92.9 23.1 %copy-start.1 = (bf16[1,128,2048]{2,1,0:T(8,128)(2,1)S(1)}, bf16[1,128,2048]{2,1,0:T(8,128)(2,1)}, u32[]{:S(2)}) copy-start(bf16[1,128,2048]{2,1,0:T(8,128)(2,1)} %param.13) | copy-start | bytes 1572868
  92.9 23.7 %copy-start.5 = (bf16[16,128]{1,0:T(8,128)(2,1)S(1)}, bf16[16,128]{1,0:T(8,128)(2,1)}, u32[]{:S(2)}) copy-start(bf16[16,128]{1,0:T(8,128)(2,1)} %param.17) | copy-start | bytes 12292
  97.8 3.6 %copy-start = (f32[512,2048]{1,0:T(8,128)S(1)}, f32[512,2048]{1,0:T(8,128)}, u32[]{:S(2)}) copy-start(f32[512,2048]{1,0:T(8,128)} %get-tuple-element.222) | copy-start | bytes 12582916 | tf_op jit(solution)/shard_map/while
  108.7 3.6 %copy-start = (f32[512,2048]{1,0:T(8,128)S(1)}, f32[512,2048]{1,0:T(8,128)}, u32[]{:S(2)}) copy-start(f32[512,2048]{1,0:T(8,128)} %get-tuple-element.222) | copy-start | bytes 12582916 | tf_op jit(solution)/shard_map/while
  116.0 34.0 %copy-start.6 = (bf16[16,128]{1,0:T(8,128)(2,1)S(1)}, bf16[16,128]{1,0:T(8,128)(2,1)}, u32[]{:S(2)}) copy-start(bf16[16,128]{1,0:T(8,128)(2,1)} %param.18) | copy-start | bytes 12292
  182.6 101.7 %copy-start.2 = (f32[16,1,128]{2,1,0:T(1,128)S(1)}, f32[16,1,128]{2,1,0:T(1,128)}, u32[]{:S(2)}) copy-start(f32[16,1,128]{2,1,0:T(1,128)} %param.19) | copy-start | bytes 24580
  182.6 101.7 %copy-start.3 = (f32[16,1,128]{2,1,0:T(1,128)S(1)}, f32[16,1,128]{2,1,0:T(1,128)}, u32[]{:S(2)}) copy-start(f32[16,1,128]{2,1,0:T(1,128)} %param.20) | copy-start | bytes 24580
  182.6 101.7 %copy-start.4 = (f32[16,1,128]{2,1,0:T(1,128)S(1)}, f32[16,1,128]{2,1,0:T(1,128)}, u32[]{:S(2)}) copy-start(f32[16,1,128]{2,1,0:T(1,128)} %param.21) | copy-start | bytes 24580
Sparse Core Ops, SparseCore 0:
  184.5 59.5 reduce-scatter.3
where the time goes:
time: 331 us
  blocking collectives  219 us (66%)
  waiting for transfers between devices  59.8 us (18%)
  matrix products  17.4 us (5%)
  between operations  14.9 us (5%)
  local copies, waits for them, and re-layouts  9.2 us (3%)
  other arithmetic  8.7 us (3%)
    reduce_scatter x1, waiting for transfers between devices, local(): lax.psum_scatter(jnp.concatenate([grad_k, grad_v], axis=1).astype(jnp.bfl...  59.8 us
    all_gather x1, blocking collectives, local(): values = lax.all_gather(document_values, 'ctx', axis=1, tiled=True)[0]  31 us
    all_gather x1, blocking collectives, local(): keys = lax.all_gather(document_keys, 'ctx', axis=1, tiled=True)[0]  30.9 us
    all_gather x1, blocking collectives, local(): lax.all_gather(cart_keys, 'ctx', axis=0, tiled=True)  30.6 us
    all_gather x1, blocking collectives, local(): lax.all_gather(cartridge_values, 'ctx', axis=0, tiled=True)  30.6 us
    all_gather x1, blocking collectives, local(): fresh = lax.all_gather(columns, 'ctx', axis=0, tiled=True)  30.5 us
    psum x1, blocking collectives, local(): squares = lax.psum(jnp.sum(full * full), ('ctx', 'head'))  30.1 us
    all_gather x1, blocking collectives, local(): all_pos = lax.all_gather(doc_pos[0], 'ctx', axis=0, tiled=True)  22.5 us
  transfers between devices with their start and end apart: 1, of which 1 were waited for; matrix products, arithmetic and copies ran while one was open for 0% of the time, Pallas kernels for 0%

commit v1 on v0

--- a/solution.py
+++ b/solution.py
@@ -133,7 +133,13 @@
     new_master = master - learn_rate * new_moment1 / (jnp.sqrt(new_moment2) + adam_eps)
     copies = new_master.reshape(master.shape[0], width).astype(jnp.bfloat16)
     columns = lax.all_gather(copies, "dp", axis=1, tiled=True)
-    fresh = lax.all_gather(columns, "ctx", axis=0, tiled=True)
+    size = lax.axis_size("ctx")
+    moving, blocks = (columns, [columns])
+    for _ in range(size - 1):
+        moving = lax.ppermute(moving, "ctx", [(i, (i + 1) % size) for i in range(size)])
+        blocks.insert(0, moving)
+    line = jnp.concatenate(blocks, axis=0)
+    fresh = jnp.roll(line, (lax.axis_index("ctx") + 1) * columns.shape[0], axis=0)
     final = combine(cart_part(fresh[:, :head_dim], fresh[:, head_dim:]), state)
     new_out = (final[2] / final[1][:, None]).astype(jnp.bfloat16).reshape(1, rows, group * head_dim)
     return (new_out, new_master, new_moment1, new_moment2)

time: 331 us -> 345 us (1.042)
  waiting for transfers between devices: 59.8 us -> 104 us
  blocking collectives: 219 us -> 189 us
    ppermute x0 -> x7, waiting for transfers between devices: none -> 44.4 us  [local(): lax.ppermute(moving, 'ctx', [(i, (i + 1) % size) for i in range(size)])]
    all_gather x1 -> x0, blocking collectives: 30.5 us -> none  [local(): fresh = lax.all_gather(columns, 'ctx', axis=0, tiled=True)]
  transfers between devices with their start and end apart: 1 -> 8, of which waited for: 1 -> 8; matrix products, arithmetic and copies ran while one was open for 0% -> 0% of each run, Pallas kernels for 0% -> 0%
where the time goes in v1:
time: 345 us
  blocking collectives  189 us (55%)
  waiting for transfers between devices  104 us (30%)
  matrix products  17.5 us (5%)
  between operations  15 us (4%)
  local copies, waits for them, and re-layouts  9.25 us (3%)
  other arithmetic  8.7 us (3%)
    reduce_scatter x1, waiting for transfers between devices, local(): lax.psum_scatter(jnp.concatenate([grad_k, grad_v], axis=1).astype(jnp.bfl...  59.7 us
    ppermute x7, waiting for transfers between devices, local(): lax.ppermute(moving, 'ctx', [(i, (i + 1) % size) for i in range(size)])  44.4 us
    all_gather x1, blocking collectives, local(): values = lax.all_gather(document_values, 'ctx', axis=1, tiled=True)[0]  31 us
    all_gather x1, blocking collectives, local(): keys = lax.all_gather(document_keys, 'ctx', axis=1, tiled=True)[0]  30.9 us
    all_gather x1, blocking collectives, local(): lax.all_gather(cart_keys, 'ctx', axis=0, tiled=True)  30.6 us
    all_gather x1, blocking collectives, local(): lax.all_gather(cartridge_values, 'ctx', axis=0, tiled=True)  30.6 us
    psum x1, blocking collectives, local(): squares = lax.psum(jnp.sum(full * full), ('ctx', 'head'))  30.1 us
    all_gather x1, blocking collectives, local(): all_pos = lax.all_gather(doc_pos[0], 'ctx', axis=0, tiled=True)  22.5 us
  transfers between devices with their start and end apart: 8, of which 8 were waited for; matrix products, arithmetic and copies ran while one was open for 0% of the time, Pallas kernels for 0%

profile of v1, /device:TPU:0, one launch (start us, length us, event | category | flops | bytes accessed | tf_op | source)
XLA Modules:
  0.0 344.8 jit_solution(4468315680308180239)
XLA Ops:
  7.2 0.0 reduce-scatter.4.cloned.1.call-start
  7.2 22.5 %all-gather = s32[1,1024]{1,0:T(1,128)S(1)} all-gather(s32[1,128]{1,0:T(1,128)} %param.16), channel_id=2, replica_groups=mesh['dp'=2,'ctx'=8,'head'=2] {'ctx'}, dimensions={1}, use_global_device_ids=true | all-gather | bytes 4608 | tf_op jit(solution)/shard_map/all_gather | solution.py:64
  29.7 30.9 %all_gather.20 = bf16[1,1024,128]{2,1,0:T(8,128)(2,1)S(1)} all-gather(bf16[1,128,128]{2,1,0:T(8,128)(2,1)} %param.14), channel_id=1, replica_groups=mesh['dp'=2,'ctx'=8,'head'=2] {'ctx'}, dimensions={1}, use_global_device_ids=true | all-gather | bytes 294912 | tf_op jit(solution)/shard_map/all_gather | solution.py:79
  60.6 1.3 reshape_squeeze.4
  61.9 31.0 %all_gather.21 = bf16[1,1024,128]{2,1,0:T(8,128)(2,1)S(1)} all-gather(bf16[1,128,128]{2,1,0:T(8,128)(2,1)} %param.15), channel_id=1, replica_groups=mesh['dp'=2,'ctx'=8,'head'=2] {'ctx'}, dimensions={1}, use_global_device_ids=true | all-gather | bytes 294912 | tf_op jit(solution)/shard_map/all_gather | solution.py:80
  92.9 23.1 %while.15 = (s32[]{:T(128)}, f32[2048]{0:T(1024)S(1)}, f32[2048]{0:T(1024)S(1)}, f32[2048,128]{1,0:T(8,128)}, s32[2]{0:T(128)S(1)}, /*index=5*/s32[1024]{0:T(102...) while((s32[]{:T(128)}, f32[2048]{0:T(1024)S(1)}, ...), condition=%wide.region_4.5_spmd.clone, body=%wide.region_1.4_spmd.clone.sunk | while | flops 554444800 | bytes 32434936 | solution.py:93
  92.9 0.8 broadcast_in_dim.101
  93.7 0.1 le.61
  93.8 0.6 dynamic_slice.45
  95.0 0.1 dynamic_slice.46
  95.1 2.7 fusion.75
  97.8 3.5 %fusion.76 = f32[2048]{0:T(1024)S(1)} fusion(f32[512,2048]{1,0:T(8,128)} %get-tuple-element.222, f32[2048]{0:T(1024)S(1)} %select_maximum_fusion.2, s32[2048]{0:T(1024)S(1)} %le.61, s32[512]{0:T(512)S(1)} %dynamic_slice.46), kind=kLoop, calls=%fused_computation.6.clone.1 | loop fusion | flops 6289408 | bytes 4220928 | tf_op jit(solution)/shard_map/while/body/eval_jaxpr/reduce_sum | solution.py:30
  101.3 0.0 copy-done
  101.3 2.5 convolution_add_fusion.4
  103.9 0.7 broadcast_in_dim.101
  104.6 0.1 le.61
  104.7 0.6 dynamic_slice.45
  105.9 0.1 dynamic_slice.46
  106.0 2.7 fusion.75
  108.7 3.5 %fusion.76 = f32[2048]{0:T(1024)S(1)} fusion(f32[512,2048]{1,0:T(8,128)} %get-tuple-element.222, f32[2048]{0:T(1024)S(1)} %select_maximum_fusion.2, s32[2048]{0:T(1024)S(1)} %le.61, s32[512]{0:T(512)S(1)} %dynamic_slice.46), kind=kLoop, calls=%fused_computation.6.clone.1 | loop fusion | flops 6289408 | bytes 4220928 | tf_op jit(solution)/shard_map/while/body/eval_jaxpr/reduce_sum | solution.py:30
  112.2 0.0 copy-done
  112.2 3.7 %convolution_add_fusion.4 = f32[2048,128]{1,0:T(8,128)} fusion(f32[512,2048]{1,0:T(8,128)S(1)} %copy-done, f32[2048]{0:T(1024)S(1)} %select_maximum_fusion.2, s32[2048]{0:T(1024)S(1)} %le.61, s32[512]{0:T(512)S(1)} %dynamic_slice.46, f32[2048,128]{1,0:T(8,128)} %get-tuple-element.242, f32[2048]{0:T(1024)S(1)} %get-tuple-element.224, ...), kind=kOutput, calls=%fused_computation.4.clone.1 | convolution fusion | flops 275513344 | bytes 6449157 | tf_op jit(solution)/shard_map/while/body/eval_jaxpr/dot_general | solution.py:31
  116.0 0.0 copy-done.1
  116.0 0.2 reshape.48
  116.2 0.3 copy.46
  116.5 0.0 copy-done.5
  116.6 30.6 %all_gather.18 = bf16[128,128]{1,0:T(8,128)(2,1)S(1)} all-gather(bf16[16,128]{1,0:T(8,128)(2,1)S(1)} %copy-done.5), channel_id=1, replica_groups=mesh['dp'=2,'ctx'=8,'head'=2] {'ctx'}, dimensions={0}, use_global_device_ids=true | all-gather | bytes 36864 | tf_op jit(solution)/shard_map/all_gather | solution.py:66
  147.2 0.3 fusion.55
  147.5 2.6 copy.45
  150.0 0.0 copy-done.6
  150.0 30.6 %all_gather.22 = bf16[128,128]{1,0:T(8,128)(2,1)S(1)} all-gather(bf16[16,128]{1,0:T(8,128)(2,1)S(1)} %copy-done.6), channel_id=1, replica_groups=mesh['dp'=2,'ctx'=8,'head'=2] {'ctx'}, dimensions={0}, use_global_device_ids=true | all-gather | bytes 36864 | tf_op jit(solution)/shard_map/all_gather | solution.py:67
  180.6 0.2 fusion.34
  180.8 1.8 multiply_reduce_fusion
  182.6 0.0 copy-start.2
  182.6 0.0 copy-start.3
  182.6 0.0 copy-start.4
  182.6 0.4 convolution_convert_fusion
  183.0 0.6 fusion.32
  183.7 0.7 copy.55
  184.4 0.0 reduce-scatter.4.cloned.1.call-update
  184.4 59.7 %reduce-scatter.4.cloned.1.call-done = bf16[16,256]{1,0:T(8,128)(2,1)} async-done(((bf16[128,256]{1,0:T(8,128)(2,1)}), bf16[16,256]{1,0:T(8,128)(2,1)}) %reduce-scatter.4.cloned.1.call-update) | async-done | bytes 8208 | tf_op jit(solution)/shard_map/reduce_scatter | solution.py:120
  244.2 8.7 %psum.14 = f32[16,256]{1,0:T(8,128)S(1)} all-reduce(bf16[16,256]{1,0:T(8,128)(2,1)} %reduce-scatter.4.cloned.1.call-done), channel_id=1, replica_groups=mesh['dp'=2,'ctx'=8,'head'=2] {'dp'}, use_global_device_ids=true, to_apply=%region_8.9 | all-reduce | flops 4096 | bytes 24576 | tf_op jit(solution)/shard_map/psum | solution.py:126
  252.9 0.6 multiply_reduce_fusion.1
  253.5 30.1 %psum.15 = f32[]{:T(128)} all-reduce(f32[]{:T(128)} %multiply_reduce_fusion.1), channel_id=1, replica_groups=mesh['dp'=2,'ctx'=8,'head'=2] {'ctx','head'}, use_global_device_ids=true, to_apply=%region_10.11 | all-reduce | flops 1 | bytes 8 | tf_op jit(solution)/shard_map/psum | solution.py:127
  284.3 0.6 fusion.53
  284.9 4.3 %all-gather.1 = bf16[16,1,256]{2,0,1:T(8,128)(2,1)S(1)} all-gather(bf16[16,1,128]{2,0,1:T(8,128)(2,1)S(1)} %get-tuple-element.138), channel_id=3, replica_groups=mesh['dp'=2,'ctx'=8,'head'=2] {'dp'}, dimensions={2}, use_global_device_ids=true | all-gather | bytes 12288 | tf_op jit(solution)/shard_map/all_gather | solution.py:135
  289.3 0.0 collective-permute-start
  289.3 6.3 %collective-permute-done = bf16[16,256]{1,0:T(8,128)(2,1)S(1)} collective-permute-done((bf16[16,256]{1,0:T(8,128)(2,1)S(1)}, bf16[16,256]{1,0:T(8,128)(2,1)S(1)}, u32[]{:S(2)}, u32[]{:S(2)}) %collective-permute-start) | collective-permute-done | bytes 8224 | tf_op jit(solution)/shard_map/ppermute | solution.py:139
  295.6 0.0 collective-permute-start.1
  295.6 6.3 %collective-permute-done.1 = bf16[16,256]{1,0:T(8,128)(2,1)S(1)} collective-permute-done((bf16[16,256]{1,0:T(8,128)(2,1)S(1)}, bf16[16,256]{1,0:T(8,128)(2,1)S(1)}, u32[]{:S(2)}, u32[]{:S(2)}) %collective-permute-start.1) | collective-permute-done | bytes 8224 | tf_op jit(solution)/shard_map/ppermute | solution.py:139
  302.0 0.0 collective-permute-start.2
  302.0 6.3 %collective-permute-done.2 = bf16[16,256]{1,0:T(8,128)(2,1)S(1)} collective-permute-done((bf16[16,256]{1,0:T(8,128)(2,1)S(1)}, bf16[16,256]{1,0:T(8,128)(2,1)S(1)}, u32[]{:S(2)}, u32[]{:S(2)}) %collective-permute-start.2) | collective-permute-done | bytes 8224 | tf_op jit(solution)/shard_map/ppermute | solution.py:139
  308.3 0.0 collective-permute-start.3
  308.3 6.3 %collective-permute-done.3 = bf16[16,256]{1,0:T(8,128)(2,1)S(1)} collective-permute-done((bf16[16,256]{1,0:T(8,128)(2,1)S(1)}, bf16[16,256]{1,0:T(8,128)(2,1)S(1)}, u32[]{:S(2)}, u32[]{:S(2)}) %collective-permute-start.3) | collective-permute-done | bytes 8224 | tf_op jit(solution)/shard_map/ppermute | solution.py:139
  314.7 0.0 collective-permute-start.4
  314.7 6.3 %collective-permute-done.4 = bf16[16,256]{1,0:T(8,128)(2,1)S(1)} collective-permute-done((bf16[16,256]{1,0:T(8,128)(2,1)S(1)}, bf16[16,256]{1,0:T(8,128)(2,1)S(1)}, u32[]{:S(2)}, u32[]{:S(2)}) %collective-permute-start.4) | collective-permute-done | bytes 8224 | tf_op jit(solution)/shard_map/ppermute | solution.py:139
  321.0 0.0 collective-permute-start.5
  321.0 6.3 %collective-permute-done.5 = bf16[16,256]{1,0:T(8,128)(2,1)S(1)} collective-permute-done((bf16[16,256]{1,0:T(8,128)(2,1)S(1)}, bf16[16,256]{1,0:T(8,128)(2,1)S(1)}, u32[]{:S(2)}, u32[]{:S(2)}) %collective-permute-start.5) | collective-permute-done | bytes 8224 | tf_op jit(solution)/shard_map/ppermute | solution.py:139
  327.4 0.0 collective-permute-start.6
  327.4 6.3 %collective-permute-done.6 = bf16[16,256]{1,0:T(8,128)(2,1)S(1)} collective-permute-done((bf16[16,256]{1,0:T(8,128)(2,1)S(1)}, bf16[16,256]{1,0:T(8,128)(2,1)S(1)}, u32[]{:S(2)}, u32[]{:S(2)}) %collective-permute-start.6) | collective-permute-done | bytes 8224 | tf_op jit(solution)/shard_map/ppermute | solution.py:139
  333.9 0.3 fusion.56
  334.2 0.2 fusion.35
  334.4 2.5 fusion.28
  336.9 1.0 reshape.47
  (39 shorter events, 0.2 us)
Async XLA Ops:
  7.2 237.0 %reduce-scatter.4.cloned.1.call-start = ((), (), s32[]{:S(2)}) async-start(), calls=%async_computation.1 | async-start | bytes 73728 | tf_op jit(solution)/shard_map/reduce_scatter | solution.py:120
  92.9 23.1 %copy-start.1 = (bf16[1,128,2048]{2,1,0:T(8,128)(2,1)S(1)}, bf16[1,128,2048]{2,1,0:T(8,128)(2,1)}, u32[]{:S(2)}) copy-start(bf16[1,128,2048]{2,1,0:T(8,128)(2,1)} %param.13) | copy-start | bytes 1572868
  92.9 23.7 %copy-start.5 = (bf16[16,128]{1,0:T(8,128)(2,1)S(1)}, bf16[16,128]{1,0:T(8,128)(2,1)}, u32[]{:S(2)}) copy-start(bf16[16,128]{1,0:T(8,128)(2,1)} %param.17) | copy-start | bytes 12292
  97.8 3.6 %copy-start = (f32[512,2048]{1,0:T(8,128)S(1)}, f32[512,2048]{1,0:T(8,128)}, u32[]{:S(2)}) copy-start(f32[512,2048]{1,0:T(8,128)} %get-tuple-element.222) | copy-start | bytes 12582916 | tf_op jit(solution)/shard_map/while
  108.7 3.6 %copy-start = (f32[512,2048]{1,0:T(8,128)S(1)}, f32[512,2048]{1,0:T(8,128)}, u32[]{:S(2)}) copy-start(f32[512,2048]{1,0:T(8,128)} %get-tuple-element.222) | copy-start | bytes 12582916 | tf_op jit(solution)/shard_map/while
  116.0 34.1 %copy-start.6 = (bf16[16,128]{1,0:T(8,128)(2,1)S(1)}, bf16[16,128]{1,0:T(8,128)(2,1)}, u32[]{:S(2)}) copy-start(bf16[16,128]{1,0:T(8,128)(2,1)} %param.18) | copy-start | bytes 12292
  182.6 101.7 %copy-start.2 = (f32[16,1,128]{2,1,0:T(1,128)S(1)}, f32[16,1,128]{2,1,0:T(1,128)}, u32[]{:S(2)}) copy-start(f32[16,1,128]{2,1,0:T(1,128)} %param.19) | copy-start | bytes 24580
  182.6 101.7 %copy-start.3 = (f32[16,1,128]{2,1,0:T(1,128)S(1)}, f32[16,1,128]{2,1,0:T(1,128)}, u32[]{:S(2)}) copy-start(f32[16,1,128]{2,1,0:T(1,128)} %param.20) | copy-start | bytes 24580
  182.6 101.7 %copy-start.4 = (f32[16,1,128]{2,1,0:T(1,128)S(1)}, f32[16,1,128]{2,1,0:T(1,128)}, u32[]{:S(2)}) copy-start(f32[16,1,128]{2,1,0:T(1,128)} %param.21) | copy-start | bytes 24580
  289.3 6.3 %collective-permute-start = (bf16[16,256]{1,0:T(8,128)(2,1)S(1)}, bf16[16,256]{1,0:T(8,128)(2,1)S(1)}, u32[]{:S(2)}, u32[]{:S(2)}) collective-permute-start(bf16[16,256]{1,0:T(8,128)(2,1)S(1)} %bitcast.55), channel_id=1, source_target_pairs={{0,2},{2,4},{4,6},{6,8},{8,10},{10,12},{12,14},{14,0},{1,3},{3,5},... | collective-permute-start | bytes 24584 | tf_op jit(solution)/shard_map/ppermute | solution.py:139
  295.6 6.3 %collective-permute-start.1 = (bf16[16,256]{1,0:T(8,128)(2,1)S(1)}, bf16[16,256]{1,0:T(8,128)(2,1)S(1)}, u32[]{:S(2)}, u32[]{:S(2)}) collective-permute-start(bf16[16,256]{1,0:T(8,128)(2,1)S(1)} %collective-permute-done), channel_id=1, source_target_pairs={{0,2},{2,4},{4,6},{6,8},{8,10},{10,12},{12,14},{14,0},{1,3},{3,5},... | collective-permute-start | bytes 24584 | tf_op jit(solution)/shard_map/ppermute | solution.py:139
  302.0 6.3 %collective-permute-start.2 = (bf16[16,256]{1,0:T(8,128)(2,1)S(1)}, bf16[16,256]{1,0:T(8,128)(2,1)S(1)}, u32[]{:S(2)}, u32[]{:S(2)}) collective-permute-start(bf16[16,256]{1,0:T(8,128)(2,1)S(1)} %collective-permute-done.1), channel_id=1, source_target_pairs={{0,2},{2,4},{4,6},{6,8},{8,10},{10,12},{12,14},{14,0},{1,3},{3,5},... | collective-permute-start | bytes 24584 | tf_op jit(solution)/shard_map/ppermute | solution.py:139
  308.3 6.3 %collective-permute-start.3 = (bf16[16,256]{1,0:T(8,128)(2,1)S(1)}, bf16[16,256]{1,0:T(8,128)(2,1)S(1)}, u32[]{:S(2)}, u32[]{:S(2)}) collective-permute-start(bf16[16,256]{1,0:T(8,128)(2,1)S(1)} %collective-permute-done.2), channel_id=1, source_target_pairs={{0,2},{2,4},{4,6},{6,8},{8,10},{10,12},{12,14},{14,0},{1,3},{3,5},... | collective-permute-start | bytes 24584 | tf_op jit(solution)/shard_map/ppermute | solution.py:139
  314.7 6.3 %collective-permute-start.4 = (bf16[16,256]{1,0:T(8,128)(2,1)S(1)}, bf16[16,256]{1,0:T(8,128)(2,1)S(1)}, u32[]{:S(2)}, u32[]{:S(2)}) collective-permute-start(bf16[16,256]{1,0:T(8,128)(2,1)S(1)} %collective-permute-done.3), channel_id=1, source_target_pairs={{0,2},{2,4},{4,6},{6,8},{8,10},{10,12},{12,14},{14,0},{1,3},{3,5},... | collective-permute-start | bytes 24584 | tf_op jit(solution)/shard_map/ppermute | solution.py:139
  321.0 6.3 %collective-permute-start.5 = (bf16[16,256]{1,0:T(8,128)(2,1)S(1)}, bf16[16,256]{1,0:T(8,128)(2,1)S(1)}, u32[]{:S(2)}, u32[]{:S(2)}) collective-permute-start(bf16[16,256]{1,0:T(8,128)(2,1)S(1)} %collective-permute-done.4), channel_id=1, source_target_pairs={{0,2},{2,4},{4,6},{6,8},{8,10},{10,12},{12,14},{14,0},{1,3},{3,5},... | collective-permute-start | bytes 24584 | tf_op jit(solution)/shard_map/ppermute | solution.py:139
  327.4 6.3 %collective-permute-start.6 = (bf16[16,256]{1,0:T(8,128)(2,1)S(1)}, bf16[16,256]{1,0:T(8,128)(2,1)S(1)}, u32[]{:S(2)}, u32[]{:S(2)}) collective-permute-start(bf16[16,256]{1,0:T(8,128)(2,1)S(1)} %collective-permute-done.5), channel_id=1, source_target_pairs={{0,2},{2,4},{4,6},{6,8},{8,10},{10,12},{12,14},{14,0},{1,3},{3,5},... | collective-permute-start | bytes 24584 | tf_op jit(solution)/shard_map/ppermute | solution.py:139
Sparse Core Ops, SparseCore 0:
  184.5 59.5 reduce-scatter.3
